TPU v7x, 32 devices: a whole 2x2x4 slice. The times are simulated.
32 devices in a mesh: dp: 8 (over y, x, core), tensor: 4 (over z).
Axes of the slice: x: 2, y: 2, z: 4, core: 2. Of those that a mesh axis runs over, the one named last changes fastest.
Arguments:
- hidden_in: bfloat16 [8, 1024, 2048], P('dp', 'tensor'), may hold values from -6 to 6
- cotangent: bfloat16 [8, 1024, 2048], P('dp', 'tensor'), may hold values from -6 to 6
- lengths: int32 [8], replicated, may hold values from 1 to 1024, 5632 in all
- slot_of_seq: int32 [8], replicated, may hold values from 0 to 7, as said below
- seq_of_slot: int32 [8], replicated, may hold values from 0 to 7, as said below
- qkv_weight: bfloat16 [2048, 3, 2048], P('dp', None, 'tensor'), may hold values from -0.125 to 0.125
- out_weight: bfloat16 [2048, 2048], P('dp', 'tensor'), may hold values from -0.75 to 0.75
- fc1_weight: bfloat16 [2048, 8192], P('dp', 'tensor'), may hold values from -0.125 to 0.125
- fc2_weight: bfloat16 [2048, 8192], P('dp', 'tensor'), may hold values from -0.0625 to 0.0625
- ln_gain: bfloat16 [2048], P(('dp', 'tensor')), may hold values from 0.5 to 1.5
- ln_bias: bfloat16 [2048], P(('dp', 'tensor')), may hold values from -3 to 3
- qkv_bias: bfloat16 [6144], P(('dp', 'tensor')), may hold values from -3 to 3
- out_bias: bfloat16 [2048], P(('dp', 'tensor')), may hold values from -3 to 3
- fc1_bias: bfloat16 [8192], P(('dp', 'tensor')), may hold values from -3 to 3
- fc2_bias: bfloat16 [2048], P(('dp', 'tensor')), may hold values from -3 to 3
Outputs:
- block_out: bfloat16 [8, 1024, 2048], P('dp', 'tensor')
- grad_input: bfloat16 [8, 1024, 2048], P('dp', 'tensor')
- grad_qkv_weight: float32 [2048, 3, 2048], P('dp', None, 'tensor')
- grad_out_weight: float32 [2048, 2048], P('dp', 'tensor')
- grad_fc1_weight: float32 [2048, 8192], P('dp', 'tensor')
- grad_fc2_weight: float32 [2048, 8192], P('dp', 'tensor')
- grad_ln_gain: float32 [2048], P(('dp', 'tensor'))
- grad_ln_bias: float32 [2048], P(('dp', 'tensor'))
- grad_qkv_bias: float32 [6144], P(('dp', 'tensor'))
- grad_out_bias: float32 [2048], P(('dp', 'tensor'))
- grad_fc1_bias: float32 [8192], P(('dp', 'tensor'))
- grad_fc2_bias: float32 [2048], P(('dp', 'tensor'))
Inputs may be any that keep to these rules, and one draw needn't show every extreme that they name: 8 lengths that sum to 5632, the longest exactly 1024; sequence s fills positions 0 to lengths[s] - 1. A permutation: sequence s is computed in slot slot_of_seq[s]; slot p lies on index p // 1 of dp. `seq_of_slot`: the inverse permutation of slot_of_seq.
All inputs are finite; a program needn't handle non-finite values.
Results may differ from a plain program's by a relative error of at most 0.0086.
Values may be sent and summed in bfloat16 or wider, within the bound.
No kernel may reach another device: no remote copies, remote signals or barrier semaphores. Data moves between devices by JAX's collectives and lax.ppermute only.
A program may use at most 256 MiB of HBM per device.

v0:
```python
import math
import jax
import jax.numpy as jnp
from jax import lax
from jax.sharding import PartitionSpec as P

HEAD_DIM = 64
ROT = 32
eps = 1e-05
masked_score = -1e30


def rotary_tables(row_count, col_count):
    half_rot = ROT // 2
    column = jnp.arange(col_count) % HEAD_DIM
    exponent = (2 * (column % half_rot)).astype(jnp.float32) / ROT
    frequency = jnp.exp(-math.log(10000.0) * exponent)
    angles = jnp.arange(row_count).astype(jnp.float32)[:, None] * frequency[None, :]
    inside = column < ROT
    cosine = jnp.where(inside, jnp.cos(angles), 1.0)
    sine_part = jnp.sin(angles)
    ahead_sin = jnp.where(column < half_rot, -sine_part, 0.0)
    behind_sin = jnp.where(inside & (column >= half_rot), sine_part, 0.0)
    return (cosine, ahead_sin, behind_sin)


def rotate(field, tables):
    cosine, ahead_sin, behind_sin = tables
    half_rot = ROT // 2
    return (
        field * cosine
        + jnp.roll(field, -half_rot, axis=-1) * ahead_sin
        + jnp.roll(field, half_rot, axis=-1) * behind_sin
    )


def pick_rows(gathered, shard_rows, wanted):
    shard_count = shard_rows.shape[0]
    inside = (wanted >= 0) & (wanted < shard_count)
    picked = jnp.take(shard_rows, jnp.clip(wanted, 0, shard_count - 1), axis=0)
    return jnp.where(inside[:, None, None], picked, gathered)


def normalize(rows_in):
    row_mean = jnp.mean(rows_in, -1, keepdims=True)
    centred = rows_in - row_mean
    variance = jnp.mean(centred * centred, -1, keepdims=True)
    inv_scale = lax.rsqrt(variance + eps)
    return (centred * inv_scale, inv_scale)


def block_scores(queries, key_heads, first_row, block_rows, length):
    head_count = key_heads.shape[1]
    query_block = queries[first_row : first_row + block_rows].reshape(
        block_rows, head_count, HEAD_DIM
    )
    scores = jnp.einsum(
        "qhd,khd->hqk", query_block, key_heads, preferred_element_type=jnp.float32
    ) * (1.0 / math.sqrt(HEAD_DIM))
    row_ids = first_row + jnp.arange(block_rows, dtype=jnp.int32)
    col_ids = jnp.arange(key_heads.shape[0], dtype=jnp.int32)
    allowed = (col_ids[None, :] <= row_ids[:, None]) & (col_ids[None, :] < length)
    return (jnp.where(allowed[None], scores, masked_score), query_block)


def attend_forward(inputs):
    queries, key_rows, values, length = inputs
    seq_len = queries.shape[0]
    head_count = queries.shape[1] // HEAD_DIM
    key_heads = key_rows.reshape(seq_len, head_count, HEAD_DIM)
    value_heads = values.reshape(seq_len, head_count, HEAD_DIM)
    block_rows = min(512, seq_len)
    mixed_parts = []
    total_parts = []
    for first_row in range(0, seq_len, block_rows):
        scores, query_block = block_scores(queries, key_heads, first_row, block_rows, length)
        row_max = jnp.max(scores, -1, keepdims=True)
        exped = jnp.exp(scores - row_max)
        row_total = jnp.sum(exped, -1, keepdims=True)
        attn_probs = (exped / row_total).astype(jnp.bfloat16)
        attention_mixture = jnp.einsum(
            "hqk,khd->qhd", attn_probs, value_heads, preferred_element_type=jnp.float32
        )
        mixed_parts.append(attention_mixture.reshape(block_rows, head_count * HEAD_DIM))
        total_parts.append(row_max[..., 0] + jnp.log(row_total[..., 0]))
    return (jnp.concatenate(mixed_parts, 0).astype(jnp.bfloat16), jnp.concatenate(total_parts, 1))


def attend_backward(inputs):
    queries, key_rows, values, log_total, grad_mixed, length = inputs
    seq_len = queries.shape[0]
    head_count = queries.shape[1] // HEAD_DIM
    key_heads = key_rows.reshape(seq_len, head_count, HEAD_DIM)
    value_heads = values.reshape(seq_len, head_count, HEAD_DIM)
    block_rows = min(512, seq_len)
    score_scale = 1.0 / math.sqrt(HEAD_DIM)
    grad_query_parts = []
    grad_keys = jnp.zeros((seq_len, head_count, HEAD_DIM), jnp.float32)
    grad_values = jnp.zeros((seq_len, head_count, HEAD_DIM), jnp.float32)
    for first_row in range(0, seq_len, block_rows):
        scores, query_block = block_scores(queries, key_heads, first_row, block_rows, length)
        attn_probs = jnp.exp(scores - log_total[:, first_row : first_row + block_rows, None])
        grad_block = grad_mixed[first_row : first_row + block_rows].reshape(
            block_rows, head_count, HEAD_DIM
        )
        grad_probs = jnp.einsum(
            "qhd,khd->hqk", grad_block, value_heads, preferred_element_type=jnp.float32
        )
        grad_scores = (
            attn_probs * (grad_probs - jnp.sum(attn_probs * grad_probs, -1, keepdims=True))
        ).astype(jnp.bfloat16)
        grad_query = (
            jnp.einsum("hqk,khd->qhd", grad_scores, key_heads, preferred_element_type=jnp.float32)
            * score_scale
        )
        grad_query_parts.append(grad_query.reshape(block_rows, head_count * HEAD_DIM))
        grad_keys = (
            grad_keys
            + jnp.einsum(
                "hqk,qhd->khd", grad_scores, query_block, preferred_element_type=jnp.float32
            )
            * score_scale
        )
        grad_values = grad_values + jnp.einsum(
            "hqk,qhd->khd",
            attn_probs.astype(jnp.bfloat16),
            grad_block,
            preferred_element_type=jnp.float32,
        )
    return (
        jnp.concatenate(grad_query_parts, 0),
        grad_keys.reshape(seq_len, head_count * HEAD_DIM),
        grad_values.reshape(seq_len, head_count * HEAD_DIM),
    )


def activations(
    layernorm_rows,
    query_key_value_whole,
    first_linear_whole,
    bias_qkv,
    first_linear_bias,
    tables,
    slot_len,
):
    qkv_raw = (
        jnp.einsum(
            "mnv,voe->mnoe",
            layernorm_rows,
            query_key_value_whole,
            preferred_element_type=jnp.float32,
        )
        + bias_qkv
    )
    queries = rotate(qkv_raw[:, :, 0], tables).astype(jnp.bfloat16)
    key_rows = rotate(qkv_raw[:, :, 1], tables).astype(jnp.bfloat16)
    values = qkv_raw[:, :, 2].astype(jnp.bfloat16)
    attention_mixture, log_total = lax.map(attend_forward, (queries, key_rows, values, slot_len))
    pre_act = (
        jnp.einsum(
            "bjp,pv->bjv", layernorm_rows, first_linear_whole, preferred_element_type=jnp.float32
        )
        + first_linear_bias
    )
    hidden = jax.nn.gelu(pre_act, approximate=True).astype(jnp.bfloat16)
    return (queries, key_rows, values, attention_mixture, log_total, pre_act, hidden)


def shards(
    hidden_in,
    cotangent,
    lengths,
    slot_of_seq,
    seq_of_slot,
    qkv_weight,
    out_weight,
    fc1_weight,
    fc2_weight,
    ln_gain,
    ln_bias,
    qkv_bias,
    out_bias,
    fc1_bias,
    fc2_bias,
):
    per_index = hidden_in.shape[0]
    rows_here = hidden_in.shape[1]
    width = hidden_in.shape[2]
    tensor_count = lax.axis_size("tensor")
    tensor_index = lax.axis_index("tensor")
    data_index = lax.axis_index("dp")
    seq_len = rows_here * tensor_count
    heads_local = qkv_weight.shape[2]
    hidden_local = fc1_weight.shape[1]
    my_slots = data_index * per_index + jnp.arange(per_index, dtype=jnp.int32)
    sources = jnp.take(seq_of_slot, my_slots)
    slot_len = jnp.take(lengths, sources)
    targets = jnp.take(slot_of_seq, my_slots)
    routed = pick_rows(
        jnp.zeros_like(hidden_in), lax.all_gather(hidden_in, "dp", axis=0, tiled=True), sources
    )
    gain_full, shift_full, qkv_bias_full, out_bias_full, fc1_bias_full, fc2_bias_full = (
        lax.all_gather(ln_gain, ("dp", "tensor"), axis=0, tiled=True),
        lax.all_gather(ln_bias, ("dp", "tensor"), axis=0, tiled=True),
        lax.all_gather(qkv_bias, ("dp", "tensor"), axis=0, tiled=True),
        lax.all_gather(out_bias, ("dp", "tensor"), axis=0, tiled=True),
        lax.all_gather(fc1_bias, ("dp", "tensor"), axis=0, tiled=True),
        lax.all_gather(fc2_bias, ("dp", "tensor"), axis=0, tiled=True),
    )
    gain_full = gain_full.astype(jnp.float32)
    bias_qkv = lax.dynamic_slice_in_dim(
        qkv_bias_full.astype(jnp.float32).reshape(3, width),
        tensor_index * heads_local,
        heads_local,
        1,
    )
    first_linear_bias = lax.dynamic_slice_in_dim(
        fc1_bias_full.astype(jnp.float32), tensor_index * hidden_local, hidden_local, 0
    )
    slot_rows = routed.astype(jnp.float32)
    normed, inv_scale = normalize(slot_rows)
    ln_local = (normed * gain_full + shift_full.astype(jnp.float32)).astype(jnp.bfloat16)
    ln_full = lax.all_gather(ln_local, "tensor", axis=1, tiled=True)
    query_key_value_whole, output_whole, first_linear_whole, fc2_full = (
        lax.all_gather(qkv_weight, "dp", axis=0, tiled=True),
        lax.all_gather(out_weight, "dp", axis=0, tiled=True),
        lax.all_gather(fc1_weight, "dp", axis=0, tiled=True),
        lax.all_gather(fc2_weight, "dp", axis=0, tiled=True),
    )
    tables = rotary_tables(seq_len, heads_local)
    queries, key_rows, values, attention_mixture, log_total, pre_act, hidden = activations(
        ln_full,
        query_key_value_whole,
        first_linear_whole,
        bias_qkv,
        first_linear_bias,
        tables,
        slot_len,
    )
    partial_value = jnp.einsum(
        "xhj,zj->xhz", attention_mixture, output_whole, preferred_element_type=jnp.float32
    ) + jnp.einsum("slf,ef->sle", hidden, fc2_full, preferred_element_type=jnp.float32)
    summed = lax.psum_scatter(partial_value, "tensor", scatter_dimension=1, tiled=True)
    positions = tensor_index * rows_here + jnp.arange(rows_here, dtype=jnp.int32)
    valid = (positions[None, :] < slot_len[:, None])[:, :, None]
    branch = summed + out_bias_full.astype(jnp.float32) + fc2_bias_full.astype(jnp.float32)
    block_out = (slot_rows + jnp.where(valid, branch, 0.0)).astype(jnp.bfloat16)
    grad_rows = jnp.where(valid, cotangent.astype(jnp.float32), 0.0)
    grad_bias = jnp.sum(grad_rows, axis=(0, 1))
    grad_low = grad_rows.astype(jnp.bfloat16)
    whole_gradient = lax.all_gather(grad_low, "tensor", axis=1, tiled=True)
    grad_mixed = jnp.einsum(
        "wix,xa->wia", whole_gradient, output_whole, preferred_element_type=jnp.float32
    ).astype(jnp.bfloat16)
    output_weight_gradient = jnp.einsum(
        "rav,rac->vc", whole_gradient, attention_mixture, preferred_element_type=jnp.float32
    )
    grad_hidden = jnp.einsum(
        "sle,ef->slf", whole_gradient, fc2_full, preferred_element_type=jnp.float32
    )
    grad_fc2_w = jnp.einsum(
        "sle,slf->ef", whole_gradient, hidden, preferred_element_type=jnp.float32
    )
    _, gelu_pull = jax.vjp(lambda inputs: jax.nn.gelu(inputs, approximate=True), pre_act)
    preactivation_gradient = gelu_pull(grad_hidden)[0].astype(jnp.bfloat16)
    grad_fc1_b = jnp.sum(preactivation_gradient, axis=(0, 1), dtype=jnp.float32)
    first_linear_weight_gradient = jnp.einsum(
        "hwj,hwy->jy", ln_full, preactivation_gradient, preferred_element_type=jnp.float32
    )
    layernorm_gradient = jnp.einsum(
        "mig,qg->miq",
        preactivation_gradient,
        first_linear_whole,
        preferred_element_type=jnp.float32,
    )
    grad_query, grad_keys, grad_values = lax.map(
        attend_backward, (queries, key_rows, values, log_total, grad_mixed, slot_len)
    )
    _, rotate_pull = jax.vjp(lambda field: rotate(field, tables), grad_query)
    query_key_value_gradient = jnp.stack(
        [rotate_pull(grad_query)[0], rotate_pull(grad_keys)[0], grad_values], axis=2
    ).astype(jnp.bfloat16)
    grad_qkv_b = jnp.sum(query_key_value_gradient, axis=(0, 1), dtype=jnp.float32)
    query_key_value_weight_gradient = jnp.einsum(
        "jqm,jqnx->mnx", ln_full, query_key_value_gradient, preferred_element_type=jnp.float32
    )
    layernorm_gradient = layernorm_gradient + jnp.einsum(
        "zrhv,nhv->zrn",
        query_key_value_gradient,
        query_key_value_whole,
        preferred_element_type=jnp.float32,
    )
    grad_ln_rows = lax.psum_scatter(layernorm_gradient, "tensor", scatter_dimension=1, tiled=True)
    grad_gain = jnp.sum(grad_ln_rows * normed, axis=(0, 1))
    grad_shift = jnp.sum(grad_ln_rows, axis=(0, 1))
    grad_norm = grad_ln_rows * gain_full
    grad_from_norm = inv_scale * (
        grad_norm
        - jnp.mean(grad_norm, -1, keepdims=True)
        - normed * jnp.mean(grad_norm * normed, -1, keepdims=True)
    )
    grad_slot = (cotangent.astype(jnp.float32) + grad_from_norm).astype(jnp.bfloat16)
    grad_input = pick_rows(
        jnp.zeros_like(grad_slot), lax.all_gather(grad_slot, "dp", axis=0, tiled=True), targets
    )
    grad_qkv_weight, grad_out_weight, grad_fc1_weight, grad_fc2_weight = (
        lax.psum_scatter(query_key_value_weight_gradient, "dp", scatter_dimension=0, tiled=True),
        lax.psum_scatter(output_weight_gradient, "dp", scatter_dimension=0, tiled=True),
        lax.psum_scatter(first_linear_weight_gradient, "dp", scatter_dimension=0, tiled=True),
        lax.psum_scatter(grad_fc2_w, "dp", scatter_dimension=0, tiled=True),
    )
    full_qkv_b = lax.dynamic_update_slice_in_dim(
        jnp.zeros((3, width), jnp.float32), grad_qkv_b, tensor_index * heads_local, 1
    ).reshape(3 * width)
    full_fc1_b = lax.dynamic_update_slice_in_dim(
        jnp.zeros((hidden_local * tensor_count,), jnp.float32),
        grad_fc1_b,
        tensor_index * hidden_local,
        0,
    )
    small_sums = (
        lax.psum_scatter(grad_gain, ("dp", "tensor"), scatter_dimension=0, tiled=True),
        lax.psum_scatter(grad_shift, ("dp", "tensor"), scatter_dimension=0, tiled=True),
        lax.psum_scatter(full_qkv_b, ("dp", "tensor"), scatter_dimension=0, tiled=True),
        lax.psum_scatter(grad_bias, ("dp", "tensor"), scatter_dimension=0, tiled=True),
        lax.psum_scatter(full_fc1_b, ("dp", "tensor"), scatter_dimension=0, tiled=True),
        lax.psum_scatter(grad_bias, ("dp", "tensor"), scatter_dimension=0, tiled=True),
    )
    return (
        block_out,
        grad_input,
        grad_qkv_weight,
        grad_out_weight,
        grad_fc1_weight,
        grad_fc2_weight,
        small_sums[0],
        small_sums[1],
        small_sums[2],
        small_sums[3],
        small_sums[4],
        small_sums[5],
    )


def solution(mesh):
    in_specs = (
        P("dp", "tensor", None),
        P("dp", "tensor", None),
        P(),
        P(),
        P(),
        P("dp", None, "tensor"),
        P("dp", "tensor"),
        P("dp", "tensor"),
        P("dp", "tensor"),
        P(("dp", "tensor")),
        P(("dp", "tensor")),
        P(("dp", "tensor")),
        P(("dp", "tensor")),
        P(("dp", "tensor")),
        P(("dp", "tensor")),
    )
    out_specs = (
        P("dp", "tensor", None),
        P("dp", "tensor", None),
        P("dp", None, "tensor"),
        P("dp", "tensor"),
        P("dp", "tensor"),
        P("dp", "tensor"),
        P(("dp", "tensor")),
        P(("dp", "tensor")),
        P(("dp", "tensor")),
        P(("dp", "tensor")),
        P(("dp", "tensor")),
        P(("dp", "tensor")),
    )
    return jax.shard_map(shards, mesh=mesh, in_specs=in_specs, out_specs=out_specs, check_vma=False)
```

profile of v0, /device:TPU:0, one launch (start us, length us, event | category | flops | bytes accessed | tf_op | source)
XLA Modules:
  0.0 1402.8 jit_solution(5798299145258276597)
XLA Ops:
  18.2 43.2 %all-reduce.19 = (bf16[2048]{0:T(1024)(128)(2,1)S(1)}, bf16[2048]{0:T(1024)(128)(2,1)S(1)}, bf16[6144]{0:T(1024)(128)(2,1)S(1)}, bf16[2048]{0:T(1024)(128)(2,1)}, bf16[2048]{0:T(1024)(128)(2,1)}) all-reduce(bf16[2048]{0:T(1024)(128)(2,1)S(1)} %dynamic-update-slice.5, ...), channel_id=1, replica_groups=mesh['dp'=8,'tensor'=4] {'dp','tensor'}, use_global_device_ids=true, to_apply=%add.9 | all-reduce | flops 14336 | bytes 57344
  77.9 68.1 %all-gather = bf16[32,1,256]{2,1,0:T(2,128)(2,1)S(1)} all-gather(bf16[1,1,256]{2,1,0:T(2,128)(2,1)S(1)} %reshape.1348), channel_id=1, replica_groups=mesh['dp'=8,'tensor'=4] {'dp','tensor'}, dimensions={0}, use_global_device_ids=true | all-gather | bytes 16896 | tf_op jit(solution)/shard_map/all_gather | solution.py:207
  148.2 33.4 %all-gather.22.cloned.1.call-done = bf16[1,1024,2048]{2,1,0:T(8,128)(2,1)} async-done(((bf16[1,256,2048]{2,1,0:T(8,128)(2,1)}), bf16[1,1024,2048]{2,1,0:T(8,128)(2,1)}) %all-gather.22.cloned.1.call-update) | async-done | bytes 4194320 | tf_op jit(solution)/shard_map/all_gather | solution.py:251
  187.8 41.3 %all-gather.14.cloned.1.call-done = bf16[2048,3,512]{0,2,1:T(8,128)(2,1)} async-done(((bf16[256,3,512]{0,2,1:T(8,128)(2,1)}), bf16[2048,3,512]{0,2,1:T(8,128)(2,1)}) %all-gather.14.cloned.1.call-update) | async-done | bytes 6291472 | tf_op jit(solution)/shard_map/all_gather | solution.py:225
  229.1 82.8 %all-gather.12.cloned.1.call-done = bf16[1,1024,2048]{2,1,0:T(8,128)(2,1)} async-done(((bf16[1,256,2048]{2,1,0:T(8,128)(2,1)}), bf16[1,1024,2048]{2,1,0:T(8,128)(2,1)}) %all-gather.12.cloned.1.call-update) | async-done | bytes 4194320 | tf_op jit(solution)/shard_map/all_gather | solution.py:223
  367.1 13.1 multiply_reduce_fusion.1
  380.2 11.9 multiply_convert_fusion.1
  414.7 10.8 multiply_convert_fusion
  466.6 14.7 %fusion.32 = f32[1024,2048]{1,0:T(8,128)} fusion(bf16[2048,2048]{1,0:T(8,128)(2,1)} %all-gather.18.cloned.1.call-done, bf16[1,1024,2048]{2,1,0:T(8,128)(2,1)} %all-gather.12.cloned.1.call-done), kind=kOutput, calls=%fused_computation.50 | convolution fusion | flops 8589934592 | bytes 20971520 | tf_op jit(solution)/shard_map/bjp,pv->bjv/dot_general | solution.py:160
  481.2 19.9 %convert_reduce_fusion = (f32[2048]{0:T(1024)S(1)}, bf16[1024,2048]{1,0:T(8,128)(2,1)}) fusion(f32[1024,2048]{1,0:T(8,128)} %fusion.32, f32[2048]{0:T(1024)S(1)} %copy-done.31, bf16[2048,2048]{1,0:T(8,128)(2,1)} %all-gather.20.cloned.1.call-done, bf16[1,1024,2048]{2,1,0:T(8,128)(2,1)} %all-gather.22.cloned.1.call-done), kind=kOutput, calls=%fused_computation.29 | convolution fusion | flops 8638167040 | bytes 25182208 | tf_op jit(solution)/shard_map/sle,ef->slf/dot_general | solution.py:258
  501.2 11.0 fusion.137
  512.2 10.8 fusion.15
  523.1 17.8 %fusion.127 = f32[1024,2048]{1,0:T(8,128)} fusion(bf16[2048,2048]{1,0:T(8,128)(2,1)} %all-gather.20.cloned.1.call-done, f32[1024,2048]{1,0:T(8,128)} %fusion.32, f32[2048]{0:T(1024)S(1)} %copy-done.31), kind=kOutput, calls=%fused_computation.183 | convolution fusion | flops 8610906112 | bytes 25174016 | tf_op jit(solution)/shard_map/slf,ef->sle/dot_general | solution.py:242
  566.4 101.0 %reduce-scatter.9.cloned.1.call-done = f32[1,256,2048]{2,1,0:T(8,128)} async-done(((f32[1,1024,2048]{2,1,0:T(8,128)}), f32[1,256,2048]{2,1,0:T(8,128)}) %reduce-scatter.9.cloned.1.call-update) | async-done | bytes 2097168 | tf_op jit(solution)/shard_map/reduce_scatter | solution.py:293
  670.9 144.1 %reduce-scatter.7.cloned.1.call-done = f32[1,256,2048]{2,1,0:T(8,128)} async-done(((f32[1,1024,2048]{2,1,0:T(8,128)}), f32[1,256,2048]{2,1,0:T(8,128)}) %reduce-scatter.7.cloned.1.call-update) | async-done | bytes 2097168 | tf_op jit(solution)/shard_map/reduce_scatter | solution.py:243
  828.3 12.0 fusion.28
  840.3 16.4 %fusion.20 = f32[2048,2048]{1,0:T(8,128)} fusion(bf16[1,1024,2048]{2,1,0:T(8,128)(2,1)} %all-gather.22.cloned.1.call-done, f32[1024,2048]{1,0:T(8,128)} %fusion.32, f32[2048]{0:T(1024)S(1)} %copy-done.31), kind=kOutput, calls=%fused_computation.38 | convolution fusion | flops 8610906112 | bytes 29368320 | tf_op jit(solution)/shard_map/sle,slf->ef/dot_general | solution.py:261
  856.7 15.2 %fusion.34 = f32[2048,2048]{1,0:T(8,128)} fusion(bf16[1024,2048]{1,0:T(8,128)(2,1)} %get-tuple-element.159, bf16[1,1024,2048]{2,1,0:T(8,128)(2,1)} %all-gather.12.cloned.1.call-done), kind=kOutput, calls=%fused_computation.52 | convolution fusion | flops 8589934592 | bytes 25165824 | tf_op jit(solution)/shard_map/hwj,hwy->jy/dot_general | solution.py:267
  873.8 70.6 %all-reduce.22.cloned.1.call-done = (f32[2048]{0:T(1024)}, f32[2048]{0:T(1024)}, f32[6144]{0:T(1024)}, f32[2048]{0:T(1024)}, f32[8192]{0:T(1024)}) async-done(((f32[2048]{0:T(1024)}, f32[2048]{0:T(1024)}, f32[6144]{0:T(1024)}, f32[2048]{0:T(1024)}, f32[8192]{0:T(1024)}), (f32[2048]{0:T(1024)}, f32[2048]{0:T(1024)}, f32[6144]{0:T(1024)}, f32[2048]{0:T(1024)}, f32[8192]{0:T(1024)})) %all-reduce.22.cloned.1.call-update) | async-done | bytes 81936
  950.3 52.3 %all-gather.24.cloned.1.call-done = bf16[8,256,2048]{2,1,0:T(8,128)(2,1)} async-done(((bf16[1,256,2048]{2,1,0:T(8,128)(2,1)}), bf16[8,256,2048]{2,1,0:T(8,128)(2,1)}) %all-gather.24.cloned.1.call-update) | async-done | bytes 8388624 | tf_op jit(solution)/shard_map/all_gather | solution.py:304
  1005.0 52.9 %reduce-scatter.13.cloned.1.call-done = f32[256,512]{1,0:T(8,128)} async-done(((f32[2048,512]{1,0:T(8,128)}), f32[256,512]{1,0:T(8,128)}) %reduce-scatter.13.cloned.1.call-update) | async-done | bytes 524304 | tf_op jit(solution)/shard_map/reduce_scatter | solution.py:308
  1057.8 96.9 %reduce-scatter.11.cloned.1.call-done = f32[256,3,512]{2,0,1:T(8,128)} async-done(((f32[2048,3,512]{2,0,1:T(8,128)}), f32[256,3,512]{2,0,1:T(8,128)}) %reduce-scatter.11.cloned.1.call-update) | async-done | bytes 1572880 | tf_op jit(solution)/shard_map/reduce_scatter | solution.py:307
  1154.7 120.4 %reduce-scatter.17.cloned.1.call-done = f32[256,2048]{1,0:T(8,128)} async-done(((f32[2048,2048]{1,0:T(8,128)}), f32[256,2048]{1,0:T(8,128)}) %reduce-scatter.17.cloned.1.call-update) | async-done | bytes 2097168 | tf_op jit(solution)/shard_map/reduce_scatter | solution.py:310
  1275.1 120.4 %reduce-scatter.15.cloned.1.call-done = f32[256,2048]{1,0:T(8,128)} async-done(((f32[2048,2048]{1,0:T(8,128)}), f32[256,2048]{1,0:T(8,128)}) %reduce-scatter.15.cloned.1.call-update) | async-done | bytes 2097168 | tf_op jit(solution)/shard_map/reduce_scatter | solution.py:309
  (253 shorter events, 204.9 us)
Async XLA Ops:
  7.2 61.3 %all-gather.10.cloned.1.call-start = ((), (), s32[]{:S(2)}) async-start(), calls=%async_computation.6 | async-start | bytes 9437184 | tf_op jit(solution)/shard_map/all_gather | solution.py:200
  8.0 140.2 %all-gather.16.cloned.1.call-start = ((), (), s32[]{:S(2)}) async-start(), calls=%async_computation.9 | async-start | bytes 2359296 | tf_op jit(solution)/shard_map/all_gather | solution.py:226
  8.7 172.8 %all-gather.22.cloned.1.call-start = ((), (), s32[]{:S(2)}) async-start(), calls=%async_computation.13 | async-start | bytes 5242880 | tf_op jit(solution)/shard_map/all_gather | solution.py:251
  15.6 213.4 %all-gather.14.cloned.1.call-start = ((), (), s32[]{:S(2)}) async-start(), calls=%async_computation.8 | async-start | bytes 7077888 | tf_op jit(solution)/shard_map/all_gather | solution.py:225
  16.9 295.0 %all-gather.12.cloned.1.call-start = ((), (), s32[]{:S(2)}) async-start(), calls=%async_computation.7 | async-start | bytes 5242880 | tf_op jit(solution)/shard_map/all_gather | solution.py:223
  75.2 391.3 %all-gather.18.cloned.1.call-start = ((), (), s32[]{:S(2)}) async-start(), calls=%async_computation.10 | async-start | bytes 9437184 | tf_op jit(solution)/shard_map/all_gather | solution.py:227
  75.8 405.4 %all-gather.20.cloned.1.call-start = ((), (), s32[]{:S(2)}) async-start(), calls=%async_computation.11 | async-start | bytes 9437184 | tf_op jit(solution)/shard_map/all_gather | solution.py:228
  76.6 590.8 %reduce-scatter.9.cloned.1.call-start = ((), (), s32[]{:S(2)}) async-start(), calls=%async_computation.14 | async-start | bytes 10485760 | tf_op jit(solution)/shard_map/reduce_scatter | solution.py:293
  76.6 248.1 %copy-start.40 = (pred[512]{0:T(512)(128)(4,1)}, pred[512]{0:T(512)(128)(4,1)S(1)}, u32[]{:S(2)}) copy-start(pred[512]{0:T(512)(128)(4,1)S(1)} %fusion.121) | copy-start | bytes 1540
  77.2 247.5 %copy-start.38 = (pred[512]{0:T(512)(128)(4,1)}, pred[512]{0:T(512)(128)(4,1)S(1)}, u32[]{:S(2)}) copy-start(pred[512]{0:T(512)(128)(4,1)S(1)} %get-tuple-element.165) | copy-start | bytes 1540
  77.2 247.5 %copy-start.42 = (pred[512]{0:T(512)(128)(4,1)}, pred[512]{0:T(512)(128)(4,1)S(1)}, u32[]{:S(2)}) copy-start(pred[512]{0:T(512)(128)(4,1)S(1)} %get-tuple-element.164) | copy-start | bytes 1540
  347.1 108.3 %copy-start = (f32[8,512,1024]{2,1,0:T(8,128)}, f32[8,512,1024]{2,1,0:T(8,128)S(1)}, u32[]{:S(2)}) copy-start(f32[8,512,1024]{2,1,0:T(8,128)S(1)} %get-tuple-element.151) | copy-start | bytes 50331652
  523.1 291.9 %reduce-scatter.7.cloned.1.call-start = ((), (), s32[]{:S(2)}) async-start(), calls=%async_computation.12 | async-start | bytes 10485760 | tf_op jit(solution)/shard_map/reduce_scatter | solution.py:243
  562.9 104.5 %copy-start.22 = (f32[2048]{0:T(1024)S(1)}, f32[2048]{0:T(1024)}, u32[]{:S(2)}) copy-start(f32[2048]{0:T(1024)} %copy-done.21) | copy-start | bytes 24580
  562.9 104.5 %copy-start.28 = (f32[256]{0:T(256)S(1)}, f32[256]{0:T(256)}, u32[]{:S(2)}) copy-start(f32[256]{0:T(256)} %copy-done.27) | copy-start | bytes 3076
  563.0 252.0 %copy-start.37 = (pred[256]{0:T(512)(128)(4,1)S(1)}, pred[256]{0:T(512)(128)(4,1)}, u32[]{:S(2)}) copy-start(pred[256]{0:T(512)(128)(4,1)} %copy-done.36) | copy-start | bytes 772
  563.0 381.4 %all-reduce.22.cloned.1.call-start = ((), (), s32[]{:S(2)}) async-start(), calls=%async_computation.20 | async-start | bytes 163840
  566.4 254.1 %copy-start.20 = (f32[8192]{0:T(1024)}, f32[8192]{0:T(1024)S(1)}, u32[]{:S(2)}) copy-start(f32[8192]{0:T(1024)S(1)} %dynamic_update_slice.20) | copy-start | bytes 98308
  820.6 182.1 %all-gather.24.cloned.1.call-start = ((), (), s32[]{:S(2)}) async-start(), calls=%async_computation.15 | async-start | bytes 9437184 | tf_op jit(solution)/shard_map/all_gather | solution.py:304
  821.3 236.5 %reduce-scatter.13.cloned.1.call-start = ((), (), s32[]{:S(2)}) async-start(), calls=%async_computation.17 | async-start | bytes 4718592 | tf_op jit(solution)/shard_map/reduce_scatter | solution.py:308
  828.2 326.5 %reduce-scatter.11.cloned.1.call-start = ((), (), s32[]{:S(2)}) async-start(), calls=%async_computation.16 | async-start | bytes 14155776 | tf_op jit(solution)/shard_map/reduce_scatter | solution.py:307
  840.3 434.9 %reduce-scatter.17.cloned.1.call-start = ((), (), s32[]{:S(2)}) async-start(), calls=%async_computation.19 | async-start | bytes 18874368 | tf_op jit(solution)/shard_map/reduce_scatter | solution.py:310
  856.7 538.8 %reduce-scatter.15.cloned.1.call-start = ((), (), s32[]{:S(2)}) async-start(), calls=%async_computation.18 | async-start | bytes 18874368 | tf_op jit(solution)/shard_map/reduce_scatter | solution.py:309
  946.4 449.6 %copy-start.56 = (f32[64]{0:T(128)}, f32[64]{0:T(128)S(1)}, u32[]{:S(2)}) copy-start(f32[64]{0:T(128)S(1)} %dynamic-slice.20) | copy-start | bytes 772
  (52 other events, 638.9 us)
Sparse Core Ops, SparseCore 0:
  10.0 58.5 all-gather.9
  70.4 27.8 all-gather.15
  100.5 80.9 all-gather.21
  183.8 45.2 all-gather.13
  231.1 80.7 all-gather.11
  313.6 52.9 all-gather.17
  368.4 54.3 all-gather.19
  523.2 144.2 reduce-scatter.8
  669.8 145.1 reduce-scatter.6
  821.2 123.1 all-reduce.21
  946.9 55.7 all-gather.23
  1006.4 51.3 reduce-scatter.12
  1062.3 92.3 reduce-scatter.10
  1159.1 115.9 reduce-scatter.16
  1279.5 115.9 reduce-scatter.14
where the time goes:
time: 1410 us; the launch traced here: 1400 us
  waiting for transfers between devices  927 us (66%)
  matrix products  227 us (16%)
  blocking collectives  111 us (8%)
  other arithmetic  94 us (7%)
  local copies, waits for them, and re-layouts  26.3 us (2%)
  between operations  17.1 us (1%)
    reduce_scatter x1, waiting for transfers between devices, shards(): lax.psum_scatter(partial_value, 'tensor', scatter_dimension=1, tiled=True)  144 us
    reduce_scatter x1, waiting for transfers between devices, shards(): lax.psum_scatter(grad_fc2_w, 'dp', scatter_dimension=0, tiled=True)  120 us
    reduce_scatter x1, waiting for transfers between devices, shards(): lax.psum_scatter(first_linear_weight_gradient, 'dp', scatter_dimension=0,...  120 us
    reduce_scatter x1, waiting for transfers between devices, shards(): lax.psum_scatter(layernorm_gradient, 'tensor', scatter_dimension=1, tiled...  101 us
    reduce_scatter x1, waiting for transfers between devices, shards(): lax.psum_scatter(query_key_value_weight_gradient, 'dp', scatter_dimension...  96.9 us
    all_gather x1, waiting for transfers between devices, shards(): ln_full = lax.all_gather(ln_local, 'tensor', axis=1, tiled=True)  82.8 us
    unnamed x16, waiting for transfers between devices  74 us
    all_gather x1, blocking collectives, shards(): lax.all_gather(fc1_bias, ('dp', 'tensor'), axis=0, tiled=True)  68.1 us
  transfers between devices with their start and end apart: 15, of which 12 were waited for; matrix products, arithmetic and copies ran while one was open for 21% of the time, Pallas kernels for 0%

commit v1 on v0

--- a/solution.py
+++ b/solution.py
@@ -1,3 +1,4 @@
+import functools
 import math
 import jax
 import jax.numpy as jnp
@@ -8,6 +9,33 @@
 ROT = 32
 eps = 1e-05
 masked_score = -1e30
+
+
+def _convert_unit(array_here, d0):
+    val2 = list(array_here.shape[1:])
+    val2[d0] *= array_here.shape[0]
+    return jnp.moveaxis(array_here, 0, d0).reshape(val2)
+
+
+def check_signs_all(own_rows, axis_id, out_dim):
+    degree = lax.axis_size(axis_id)
+    series = tuple(((num, (num + 1) % degree) for num in range(degree)))
+    gallery = tuple(((i0, kk) for kk, i0 in series))
+    left_arr, e_now = ([], [])
+    for w in range(degree - 1):
+        if w % 2 == 0:
+            left_arr.append(
+                lax.ppermute(left_arr[-1] if left_arr else own_rows, axis_id, perm=series)
+            )
+        else:
+            e_now.append(lax.ppermute(e_now[-1] if e_now else own_rows, axis_id, gallery))
+    d_next = jnp.stack([*left_arr[::-1], own_rows, *e_now])
+    arr_next = lax.axis_index(axis_id) - len(left_arr)
+    d_next = d_next[(jnp.arange(degree) - arr_next) % degree]
+    return _convert_unit(d_next, out_dim)
+
+
+replace_the_patch = functools.partial(check_signs_all, axis_id="tensor", out_dim=1)
 
 
 def rotary_tables(row_count, col_count):
@@ -248,7 +276,7 @@
     grad_rows = jnp.where(valid, cotangent.astype(jnp.float32), 0.0)
     grad_bias = jnp.sum(grad_rows, axis=(0, 1))
     grad_low = grad_rows.astype(jnp.bfloat16)
-    whole_gradient = lax.all_gather(grad_low, "tensor", axis=1, tiled=True)
+    whole_gradient = replace_the_patch(grad_low)
     grad_mixed = jnp.einsum(
         "wix,xa->wia", whole_gradient, output_whole, preferred_element_type=jnp.float32
     ).astype(jnp.bfloat16)

time: 1410 us -> 1330 us (0.943)
  waiting for transfers between devices: 927 us -> 793 us
  blocking collectives: 111 us -> 147 us
    all_gather x1, waiting for transfers between devices: 82.8 us -> 3.83 us  [shards(): ln_full = lax.all_gather(ln_local, 'tensor', axis=1, tiled=True)]
    all_gather x1, waiting for transfers between devices: 41.3 us -> 0.01 us  [shards(): lax.all_gather(qkv_weight, 'dp', axis=0, tiled=True)]
    all_gather x1, blocking collectives: 68.1 us -> 104 us  [shards(): lax.all_gather(fc1_bias, ('dp', 'tensor'), axis=0, tiled=True)]
    all_gather x1 -> x0, waiting for transfers between devices: 33.4 us -> none  [shards(): whole_gradient = lax.all_gather(grad_low, 'tensor', axis=1, tiled=True)]
    ppermute x0 -> x3, waiting for transfers between devices: none -> 22.7 us  [the longest x2 22.7 us: check_signs_all(): lax.ppermute(left_arr[-1] if left_arr else own_rows, axis_id, perm=series)]
    unnamed x16 -> x15, waiting for transfers between devices: 74 us -> 72 us
  transfers between devices with their start and end apart: 15 -> 17, of which waited for: 12 -> 11; matrix products, arithmetic and copies ran while one was open for 21% -> 23% of each run, Pallas kernels for 0% -> 0%
where the time goes in v1:
time: 1330 us; the launch traced here: 1320 us
  waiting for transfers between devices  793 us (60%)
  matrix products  227 us (17%)
  blocking collectives  147 us (11%)
  other arithmetic  97 us (7%)
  local copies, waits for them, and re-layouts  35 us (3%)
  between operations  17.1 us (1%)
    reduce_scatter x1, waiting for transfers between devices, shards(): lax.psum_scatter(partial_value, 'tensor', scatter_dimension=1, tiled=True)  144 us
    reduce_scatter x1, waiting for transfers between devices, shards(): lax.psum_scatter(grad_fc2_w, 'dp', scatter_dimension=0, tiled=True)  121 us
    reduce_scatter x1, waiting for transfers between devices, shards(): lax.psum_scatter(first_linear_weight_gradient, 'dp', scatter_dimension=0,...  120 us
    all_gather x1, blocking collectives, shards(): lax.all_gather(fc1_bias, ('dp', 'tensor'), axis=0, tiled=True)  104 us
    reduce_scatter x1, waiting for transfers between devices, shards(): lax.psum_scatter(layernorm_gradient, 'tensor', scatter_dimension=1, tiled...  99.9 us
    reduce_scatter x1, waiting for transfers between devices, shards(): lax.psum_scatter(query_key_value_weight_gradient, 'dp', scatter_dimension...  96.8 us
    unnamed x15, waiting for transfers between devices  72 us
    reduce_scatter x1, waiting for transfers between devices, shards(): lax.psum_scatter(output_weight_gradient, 'dp', scatter_dimension=0, tiled...  53 us
  transfers between devices with their start and end apart: 17, of which 11 were waited for; matrix products, arithmetic and copies ran while one was open for 23% of the time, Pallas kernels for 0%

profile of v1, /device:TPU:0, one launch (start us, length us, event | category | flops | bytes accessed | tf_op | source)
XLA Modules:
  0.0 1321.3 jit_solution(426264339516935768)
XLA Ops:
  17.3 43.2 %all-reduce.19 = (bf16[2048]{0:T(1024)(128)(2,1)S(1)}, bf16[2048]{0:T(1024)(128)(2,1)S(1)}, bf16[6144]{0:T(1024)(128)(2,1)S(1)}, bf16[2048]{0:T(1024)(128)(2,1)}, bf16[2048]{0:T(1024)(128)(2,1)}) all-reduce(bf16[2048]{0:T(1024)(128)(2,1)S(1)} %dynamic-update-slice.5, ...), channel_id=1, replica_groups=mesh['dp'=8,'tensor'=4] {'dp','tensor'}, use_global_device_ids=true, to_apply=%add.9 | all-reduce | flops 14336 | bytes 57344
  82.5 22.7 %collective-permute-done = bf16[1,256,2048]{2,1,0:T(8,128)(2,1)S(1)} collective-permute-done((bf16[1,256,2048]{2,1,0:T(8,128)(2,1)S(1)}, bf16[1,256,2048]{2,1,0:T(8,128)(2,1)S(1)}, u32[]{:S(2)}, u32[]{:S(2)}) %collective-permute-start) | collective-permute-done | bytes 1048608 | tf_op jit(solution)/shard_map/ppermute | solution.py:28
  105.2 104.1 %all-gather = bf16[32,1,256]{2,1,0:T(2,128)(2,1)S(1)} all-gather(bf16[1,1,256]{2,1,0:T(2,128)(2,1)S(1)} %reshape.1412), channel_id=1, replica_groups=mesh['dp'=8,'tensor'=4] {'dp','tensor'}, dimensions={0}, use_global_device_ids=true | all-gather | bytes 16896 | tf_op jit(solution)/shard_map/all_gather | solution.py:235
  230.4 10.1 add_bitcast_fusion.1
  285.6 13.1 multiply_reduce_fusion.1
  298.7 12.3 multiply_convert_fusion.1
  333.7 10.4 multiply_convert_fusion
  364.5 9.6 fusion.71
  385.2 14.5 %fusion.24 = f32[1024,2048]{1,0:T(8,128)} fusion(bf16[2048,2048]{1,0:T(8,128)(2,1)} %all-gather.17.cloned.1.call-done, bf16[1,1024,2048]{2,1,0:T(8,128)(2,1)} %all-gather.11.cloned.1.call-done), kind=kOutput, calls=%fused_computation.44 | convolution fusion | flops 8589934592 | bytes 20971520 | tf_op jit(solution)/shard_map/bjp,pv->bjv/dot_general | solution.py:188
  399.8 19.9 %convert_reduce_fusion = (f32[2048]{0:T(1024)S(1)}, bf16[1024,2048]{1,0:T(8,128)(2,1)}) fusion(f32[1024,2048]{1,0:T(8,128)} %fusion.24, f32[2048]{0:T(1024)S(1)} %copy-done.32, bf16[1024,2048]{1,0:T(8,128)(2,1)} %bitcast.153, bf16[2048,2048]{1,0:T(8,128)(2,1)} %all-gather.19.cloned.1.call-done), kind=kOutput, calls=%fused_computation.30 | convolution fusion | flops 8638167040 | bytes 25182208 | tf_op jit(solution)/shard_map/sle,ef->slf/dot_general | solution.py:286
  419.7 10.8 fusion.127
  430.6 11.0 fusion.15
  441.7 18.1 %fusion.116 = f32[1024,2048]{1,0:T(8,128)} fusion(bf16[2048,2048]{1,0:T(8,128)(2,1)} %all-gather.19.cloned.1.call-done, f32[1024,2048]{1,0:T(8,128)} %fusion.24, f32[2048]{0:T(1024)S(1)} %copy-done.32), kind=kOutput, calls=%fused_computation.186 | convolution fusion | flops 8610906112 | bytes 25174016 | tf_op jit(solution)/shard_map/slf,ef->sle/dot_general | solution.py:270
  485.9 99.9 %reduce-scatter.9.cloned.1.call-done = f32[1,256,2048]{2,1,0:T(8,128)} async-done(((f32[1,1024,2048]{2,1,0:T(8,128)}), f32[1,256,2048]{2,1,0:T(8,128)}) %reduce-scatter.9.cloned.1.call-update) | async-done | bytes 2097168 | tf_op jit(solution)/shard_map/reduce_scatter | solution.py:321
  589.4 144.1 %reduce-scatter.7.cloned.1.call-done = f32[1,256,2048]{2,1,0:T(8,128)} async-done(((f32[1,1024,2048]{2,1,0:T(8,128)}), f32[1,256,2048]{2,1,0:T(8,128)}) %reduce-scatter.7.cloned.1.call-update) | async-done | bytes 2097168 | tf_op jit(solution)/shard_map/reduce_scatter | solution.py:271
  747.6 11.9 fusion.20
  759.6 16.6 %fusion.115 = f32[2048,2048]{1,0:T(8,128)} fusion(bf16[1024,2048]{1,0:T(8,128)(2,1)} %bitcast.155, f32[1024,2048]{1,0:T(8,128)} %fusion.24, f32[2048]{0:T(1024)S(1)} %copy-done.32), kind=kOutput, calls=%fused_computation.185 | convolution fusion | flops 8610906112 | bytes 29368320 | tf_op jit(solution)/shard_map/sle,slf->ef/dot_general | solution.py:289
  776.3 15.3 %fusion.26 = f32[2048,2048]{1,0:T(8,128)} fusion(bf16[1024,2048]{1,0:T(8,128)(2,1)} %get-tuple-element.123, bf16[1,1024,2048]{2,1,0:T(8,128)(2,1)} %all-gather.11.cloned.1.call-done), kind=kOutput, calls=%fused_computation.46 | convolution fusion | flops 8589934592 | bytes 25165824 | tf_op jit(solution)/shard_map/hwj,hwy->jy/dot_general | solution.py:295
  793.5 69.4 %all-reduce.22.cloned.1.call-done = (f32[2048]{0:T(1024)}, f32[2048]{0:T(1024)}, f32[6144]{0:T(1024)}, f32[2048]{0:T(1024)}, f32[8192]{0:T(1024)}) async-done(((f32[2048]{0:T(1024)}, f32[2048]{0:T(1024)}, f32[6144]{0:T(1024)}, f32[2048]{0:T(1024)}, f32[8192]{0:T(1024)}), (f32[2048]{0:T(1024)}, f32[2048]{0:T(1024)}, f32[6144]{0:T(1024)}, f32[2048]{0:T(1024)}, f32[8192]{0:T(1024)})) %all-reduce.22.cloned.1.call-update) | async-done | bytes 81936
  868.8 52.2 %all-gather.21.cloned.1.call-done = bf16[8,256,2048]{2,1,0:T(8,128)(2,1)} async-done(((bf16[1,256,2048]{2,1,0:T(8,128)(2,1)}), bf16[8,256,2048]{2,1,0:T(8,128)(2,1)}) %all-gather.21.cloned.1.call-update) | async-done | bytes 8388624 | tf_op jit(solution)/shard_map/all_gather | solution.py:332
  923.3 53.0 %reduce-scatter.13.cloned.1.call-done = f32[256,512]{1,0:T(8,128)} async-done(((f32[2048,512]{1,0:T(8,128)}), f32[256,512]{1,0:T(8,128)}) %reduce-scatter.13.cloned.1.call-update) | async-done | bytes 524304 | tf_op jit(solution)/shard_map/reduce_scatter | solution.py:336
  976.3 96.8 %reduce-scatter.11.cloned.1.call-done = f32[256,3,512]{2,0,1:T(8,128)} async-done(((f32[2048,3,512]{2,0,1:T(8,128)}), f32[256,3,512]{2,0,1:T(8,128)}) %reduce-scatter.11.cloned.1.call-update) | async-done | bytes 1572880 | tf_op jit(solution)/shard_map/reduce_scatter | solution.py:335
  1073.1 120.6 %reduce-scatter.17.cloned.1.call-done = f32[256,2048]{1,0:T(8,128)} async-done(((f32[2048,2048]{1,0:T(8,128)}), f32[256,2048]{1,0:T(8,128)}) %reduce-scatter.17.cloned.1.call-update) | async-done | bytes 2097168 | tf_op jit(solution)/shard_map/reduce_scatter | solution.py:338
  1193.6 120.4 %reduce-scatter.15.cloned.1.call-done = f32[256,2048]{1,0:T(8,128)} async-done(((f32[2048,2048]{1,0:T(8,128)}), f32[256,2048]{1,0:T(8,128)}) %reduce-scatter.15.cloned.1.call-update) | async-done | bytes 2097168 | tf_op jit(solution)/shard_map/reduce_scatter | solution.py:337
  (255 shorter events, 204.2 us)
Async XLA Ops:
  7.2 61.2 %all-gather.9.cloned.1.call-start = ((), (), s32[]{:S(2)}) async-start(), calls=%async_computation.6 | async-start | bytes 9437184 | tf_op jit(solution)/shard_map/all_gather | solution.py:228
  7.9 212.4 %all-gather.15.cloned.1.call-start = ((), (), s32[]{:S(2)}) async-start(), calls=%async_computation.9 | async-start | bytes 2359296 | tf_op jit(solution)/shard_map/all_gather | solution.py:254
  8.7 217.9 %all-gather.13.cloned.1.call-start = ((), (), s32[]{:S(2)}) async-start(), calls=%async_computation.8 | async-start | bytes 7077888 | tf_op jit(solution)/shard_map/all_gather | solution.py:253
  11.1 219.3 %all-gather.11.cloned.1.call-start = ((), (), s32[]{:S(2)}) async-start(), calls=%async_computation.7 | async-start | bytes 5242880 | tf_op jit(solution)/shard_map/all_gather | solution.py:251
  75.1 310.1 %all-gather.17.cloned.1.call-start = ((), (), s32[]{:S(2)}) async-start(), calls=%async_computation.10 | async-start | bytes 9437184 | tf_op jit(solution)/shard_map/all_gather | solution.py:255
  75.7 324.1 %all-gather.19.cloned.1.call-start = ((), (), s32[]{:S(2)}) async-start(), calls=%async_computation.11 | async-start | bytes 9437184 | tf_op jit(solution)/shard_map/all_gather | solution.py:256
  77.3 27.9 %collective-permute-start = (bf16[1,256,2048]{2,1,0:T(8,128)(2,1)S(1)}, bf16[1,256,2048]{2,1,0:T(8,128)(2,1)S(1)}, u32[]{:S(2)}, u32[]{:S(2)}) collective-permute-start(bf16[1,256,2048]{2,1,0:T(8,128)(2,1)S(1)} %fusion.36), channel_id=1, source_target_pairs={{0,1},{1,2},{2,3},{3,0},{4,5},{5,6},{6,7},{7,4},{8,9},{9,10},{10,1... | collective-permute-start | bytes 3145736 | tf_op jit(solution)/shard_map/ppermute | solution.py:28
  78.8 132.8 %collective-permute-start.2 = (bf16[1,256,2048]{2,1,0:T(8,128)(2,1)S(1)}, bf16[1,256,2048]{2,1,0:T(8,128)(2,1)}, u32[]{:S(2)}, u32[]{:S(2)}) collective-permute-start(bf16[1,256,2048]{2,1,0:T(8,128)(2,1)S(1)} %fusion.36), channel_id=1, source_target_pairs={{1,0},{2,1},{3,2},{0,3},{5,4},{6,5},{7,6},{4,7},{9,8},{10,9},{11,1... | collective-permute-start | bytes 3145736 | tf_op jit(solution)/shard_map/ppermute | solution.py:31
  81.2 504.6 %reduce-scatter.9.cloned.1.call-start = ((), (), s32[]{:S(2)}) async-start(), calls=%async_computation.13 | async-start | bytes 10485760 | tf_op jit(solution)/shard_map/reduce_scatter | solution.py:321
  81.3 161.8 %copy-start.41 = (pred[512]{0:T(512)(128)(4,1)}, pred[512]{0:T(512)(128)(4,1)S(1)}, u32[]{:S(2)}) copy-start(pred[512]{0:T(512)(128)(4,1)S(1)} %fusion.107) | copy-start | bytes 1540
  81.9 161.2 %copy-start.39 = (pred[512]{0:T(512)(128)(4,1)}, pred[512]{0:T(512)(128)(4,1)S(1)}, u32[]{:S(2)}) copy-start(pred[512]{0:T(512)(128)(4,1)S(1)} %get-tuple-element.165) | copy-start | bytes 1540
  81.9 161.3 %copy-start.43 = (pred[512]{0:T(512)(128)(4,1)}, pred[512]{0:T(512)(128)(4,1)S(1)}, u32[]{:S(2)}) copy-start(pred[512]{0:T(512)(128)(4,1)S(1)} %get-tuple-element.164) | copy-start | bytes 1540
  105.2 106.5 %collective-permute-start.1 = (bf16[1,256,2048]{2,1,0:T(8,128)(2,1)S(1)}, bf16[1,256,2048]{2,1,0:T(8,128)(2,1)}, u32[]{:S(2)}, u32[]{:S(2)}) collective-permute-start(bf16[1,256,2048]{2,1,0:T(8,128)(2,1)S(1)} %collective-permute-done), channel_id=1, source_target_pairs={{0,1},{1,2},{2,3},{3,0},{4,5},{5,6},{6,7},{7,4},{8,9},{9,10},{10,1... | collective-permute-start | bytes 3145736 | tf_op jit(solution)/shard_map/ppermute | solution.py:28
  441.6 291.8 %reduce-scatter.7.cloned.1.call-start = ((), (), s32[]{:S(2)}) async-start(), calls=%async_computation.12 | async-start | bytes 10485760 | tf_op jit(solution)/shard_map/reduce_scatter | solution.py:271
  481.8 251.6 %copy-start.4 = (bf16[1,256,2048]{2,1,0:T(8,128)(2,1)S(1)}, bf16[1,256,2048]{2,1,0:T(8,128)(2,1)}, u32[]{:S(2)}) copy-start(bf16[1,256,2048]{2,1,0:T(8,128)(2,1)} %param.18) | copy-start | bytes 3145732
  481.8 251.6 %copy-start.34 = (pred[256]{0:T(512)(128)(4,1)S(1)}, pred[256]{0:T(512)(128)(4,1)}, u32[]{:S(2)}) copy-start(pred[256]{0:T(512)(128)(4,1)} %copy-done.33) | copy-start | bytes 772
  481.9 381.1 %all-reduce.22.cloned.1.call-start = ((), (), s32[]{:S(2)}) async-start(), calls=%async_computation.19 | async-start | bytes 163840
  485.9 252.9 %copy-start.21 = (f32[8192]{0:T(1024)}, f32[8192]{0:T(1024)S(1)}, u32[]{:S(2)}) copy-start(f32[8192]{0:T(1024)S(1)} %dynamic_update_slice.20) | copy-start | bytes 98308
  738.8 182.2 %all-gather.21.cloned.1.call-start = ((), (), s32[]{:S(2)}) async-start(), calls=%async_computation.14 | async-start | bytes 9437184 | tf_op jit(solution)/shard_map/all_gather | solution.py:332
  739.4 236.9 %reduce-scatter.13.cloned.1.call-start = ((), (), s32[]{:S(2)}) async-start(), calls=%async_computation.16 | async-start | bytes 4718592 | tf_op jit(solution)/shard_map/reduce_scatter | solution.py:336
  746.4 326.7 %reduce-scatter.11.cloned.1.call-start = ((), (), s32[]{:S(2)}) async-start(), calls=%async_computation.15 | async-start | bytes 14155776 | tf_op jit(solution)/shard_map/reduce_scatter | solution.py:335
  759.5 434.1 %reduce-scatter.17.cloned.1.call-start = ((), (), s32[]{:S(2)}) async-start(), calls=%async_computation.18 | async-start | bytes 18874368 | tf_op jit(solution)/shard_map/reduce_scatter | solution.py:338
  776.2 537.8 %reduce-scatter.15.cloned.1.call-start = ((), (), s32[]{:S(2)}) async-start(), calls=%async_computation.17 | async-start | bytes 18874368 | tf_op jit(solution)/shard_map/reduce_scatter | solution.py:337
  864.9 449.6 %copy-start.53 = (f32[64]{0:T(128)}, f32[64]{0:T(128)S(1)}, u32[]{:S(2)}) copy-start(f32[64]{0:T(128)S(1)} %dynamic-slice.20) | copy-start | bytes 772
  (51 other events, 1073.7 us)
Sparse Core Ops, SparseCore 0:
  9.9 58.4 all-gather.8
  70.3 27.9 all-gather.14
  100.7 46.6 all-gather.12
  149.4 80.9 all-gather.10
  232.2 53.0 all-gather.16
  287.0 54.3 all-gather.18
  441.7 144.0 reduce-scatter.8
  588.2 145.1 reduce-scatter.6
  739.9 123.0 all-reduce.21
  865.2 55.7 all-gather.20
  925.0 51.3 reduce-scatter.12
  980.7 92.3 reduce-scatter.10
  1077.7 115.9 reduce-scatter.16
  1198.1 115.9 reduce-scatter.14
